TPU v7x, 128 devices: a whole 4x4x4 slice. The times are simulated.
128 devices in a mesh: space: 16 (over z, x_lo, core), samp: 8 (over y, x_hi).
Axes of the slice: x: 4 (x_hi: 2, x_lo: 2; x = x_hi * 2 + x_lo), y: 4, z: 4, core: 2. Of those that a mesh axis runs over, the one named last changes fastest.
Arguments:
- basis_u: bfloat16 [128, 32, 8, 128], P('samp', 'space'), may hold values from -0.75 to 0.75
- basis_v: bfloat16 [128, 65536], P('space', 'samp'), may hold values from -0.75 to 0.75
- core_s: float32 [128, 128], replicated, may hold values from -4 to 4
- face_class: int32 [6, 32, 8, 128], P(None, 'space'), may hold values from 0 to 3
- sample_class: int32 [65536], P('samp'), may hold values from 0 to 3
Outputs:
- k_new: float32 [128, 32, 8, 128], P('samp', 'space')
- l_new: float32 [128, 65536], P('space', 'samp')
All inputs are finite; a program needn't handle non-finite values.
Results may differ from a plain program's by a relative error of at most 0.0046.
Values may be sent and summed in bfloat16 or wider, within the bound.
No kernel may reach another device: no remote copies, remote signals or barrier semaphores. Data moves between devices by JAX's collectives and lax.ppermute only.
A program may use at most 64 MiB of HBM per device.

v0:
```python
import jax
import jax.numpy as jnp
from jax import lax
from jax.sharding import PartitionSpec as P

step_size = 0.1


def padded(cells, sides, width):
    for axis, dim in sides:
        count = lax.axis_size(axis)
        ends = count - 1
        head = lax.slice_in_dim(cells, 0, width, axis=dim)
        tail = lax.slice_in_dim(cells, cells.shape[dim] - width, cells.shape[dim], axis=dim)
        cells = jnp.concatenate(
            [
                lax.ppermute(tail, axis, [(i, (i + 1) % count) for i in range(ends)]),
                cells,
                lax.ppermute(head, axis, [((i + 1) % count, i) for i in range(ends)]),
            ],
            axis=dim,
        )
    return cells


def with_core(factor, core_b):
    rank_size = core_b.shape[0]
    flat_rows = factor.reshape(rank_size, -1)
    product = lax.dot_general(
        core_b, flat_rows, (((0,), (0,)), ((), ())), preferred_element_type=jnp.float32
    ).astype(jnp.bfloat16)
    return product.reshape(factor.shape)


def diffuse(padded_k, face_class):
    weight = 0.25 * jnp.exp2(face_class.astype(jnp.float32))[:, None]
    padded_grid = jnp.pad(padded_k.astype(jnp.float32), ((0, 0), (0, 0), (1, 1), (1, 1)))
    centre = padded_grid[:, 1:-1, 1:-1, 1:-1]
    beside_all = (
        padded_grid[:, :-2, 1:-1, 1:-1],
        padded_grid[:, 2:, 1:-1, 1:-1],
        padded_grid[:, 1:-1, :-2, 1:-1],
        padded_grid[:, 1:-1, 2:, 1:-1],
        padded_grid[:, 1:-1, 1:-1, :-2],
        padded_grid[:, 1:-1, 1:-1, 2:],
    )
    summed = jnp.zeros_like(centre)
    for side_index in range(6):
        summed = summed + weight[side_index] * (beside_all[side_index] - centre)
    return summed


def per_device(basis_u, basis_v, core_s, face_class, sample_class):
    n_space = lax.axis_size("space")
    n_samp = lax.axis_size("samp")
    narrow, depth_x, rows_y, cols_z = basis_u.shape
    rank_size = core_s.shape[0]
    core_b = core_s.astype(jnp.bfloat16)
    full_u = lax.all_gather(basis_u, "samp", axis=0, tiled=True)
    k_old = with_core(full_u, core_b)
    padded_k = padded(k_old, (("space", 1),), 1)
    laplace = diffuse(padded_k, face_class)
    cells_total = depth_x * rows_y * cols_z * n_space
    samp_rows = basis_v.shape[1]
    samples_total = samp_rows * n_samp
    lane_width = rank_size // n_space
    full_v = lax.all_gather(basis_v, "space", axis=0, tiled=True)
    k_flat = k_old.reshape(rank_size, -1)
    u_rows = full_u.reshape(rank_size, -1)
    lap_b = laplace.reshape(rank_size, -1).astype(jnp.bfloat16)
    moment_part = lax.dot_general(
        u_rows, lap_b, (((1,), (1,)), ((), ())), preferred_element_type=jnp.float32
    )
    moment = lax.psum(moment_part, "space")
    growth = 0.5 + 0.5 * sample_class.astype(jnp.float32)
    block_rows = min(256, samp_rows)
    block_count = samp_rows // block_rows
    cell_weight = rank_size / cells_total

    def tile_terms(offset):
        v_block = lax.dynamic_slice_in_dim(full_v, offset, block_rows, 1)
        g_block = lax.dynamic_slice_in_dim(growth, offset, block_rows, 0)
        sample_field = lax.dot_general(
            k_flat, v_block, (((0,), (0,)), ((), ())), preferred_element_type=jnp.float32
        )
        reaction = (
            g_block[None, :] * sample_field - sample_field * sample_field * sample_field
        ).astype(jnp.bfloat16)
        onto_v = lax.dot_general(
            v_block, reaction, (((1,), (1,)), ((), ())), preferred_element_type=jnp.float32
        )
        onto_u = lax.dot_general(
            u_rows, reaction, (((1,), (0,)), ((), ())), preferred_element_type=jnp.float32
        )
        return (onto_v, onto_u * cell_weight)

    start_acc = jnp.zeros((rank_size, k_flat.shape[1]), jnp.float32)

    def turn_after(turn_index, state_pair):
        accumulated, l_terms = state_pair
        offset = turn_index * block_rows
        onto_v, l_term = tile_terms(offset)
        l_terms = lax.dynamic_update_slice_in_dim(l_terms, l_term, offset, 1)
        return (accumulated + onto_v, l_terms)

    start_terms = jnp.zeros((rank_size, samp_rows), jnp.float32)
    accumulated, l_terms = lax.fori_loop(0, block_count, turn_after, (start_acc, start_terms))
    l_proj = lax.psum_scatter(l_terms, "space", scatter_dimension=0, tiled=True)
    samp_offset = lax.axis_index("samp") * narrow
    k_term = accumulated.reshape(rank_size, depth_x, rows_y, cols_z)
    k_summed = lax.psum(k_term, "samp")
    k_proj = lax.dynamic_slice_in_dim(k_summed, samp_offset, narrow, 0)
    k_proj = k_proj * (rank_size / samples_total)
    k_mine = lax.dynamic_slice_in_dim(k_old, samp_offset, narrow, 0).astype(jnp.float32)
    lap_mine = lax.dynamic_slice_in_dim(laplace, samp_offset, narrow, 0)
    k_new = k_mine + step_size * (lap_mine + k_proj)
    lane_offset = lax.axis_index("space") * lane_width
    core_rows = lax.dynamic_slice_in_dim(core_b, lane_offset, lane_width, 0)
    l_old = jnp.dot(core_rows, full_v, preferred_element_type=jnp.float32)
    moment_rows = lax.dynamic_slice_in_dim(moment, lane_offset, lane_width, 0) * cell_weight
    side_term = jnp.dot(moment_rows, full_v.astype(jnp.float32), precision=lax.Precision.HIGHEST)
    l_new = l_old + step_size * (side_term + l_proj)
    return (k_new, l_new)


def solution(mesh):
    placed = (
        P("samp", "space", None, None),
        P("space", "samp"),
        P(),
        P(None, "space", None, None),
        P("samp"),
    )
    return jax.shard_map(
        per_device,
        mesh=mesh,
        in_specs=placed,
        out_specs=(P("samp", "space", None, None), P("space", "samp")),
        check_vma=False,
    )
```

profile of v0, /device:TPU:0, one launch (start us, length us, event | category | flops | bytes accessed | tf_op | source)
XLA Modules:
  0.0 497.0 jit_solution(16505963637963926047)
XLA Ops:
  8.8 37.5 %all_gather.6 = bf16[128,2,8,128]{3,2,1,0:T(8,128)(2,1)S(1)} all-gather(bf16[16,2,8,128]{3,2,1,0:T(8,128)(2,1)} %param.7), channel_id=1, replica_groups=mesh['space'=16,'samp'=8] {'samp'}, dimensions={0}, use_global_device_ids=true | all-gather | bytes 589824 | tf_op jit(solution)/shard_map/all_gather | solution.py:59
  50.6 3.8 collective-permute-start
  55.2 2.4 broadcast_in_dim.11.clone
  57.6 155.9 %while.16 = (s32[]{:T(128)}, f32[128,2048]{1,0:T(8,128)S(1)}, f32[128,8192]{1,0:T(8,128)}, bf16[128,8192]{1,0:T(8,128)(2,1)}, f32[8192]{0:T(1024)}, /*index=5*/b...) while((s32[]{:T(128)}, f32[128,2048]{1,0:T(8,128)S(1)}, ...), condition=%wide.region_1.2_spmd.clone, body=%wide.region_0.1_spmd.clone.sunk | while | flops 405831680 | bytes 7081149 | solution.py:107
  58.4 1.6 fusion.58
  63.2 1.6 fusion.58
  68.1 1.6 fusion.58
  73.0 1.6 fusion.58
  97.4 1.6 fusion.58
  102.3 1.6 fusion.58
  116.8 1.6 fusion.58
  131.4 1.6 fusion.58
  146.0 1.6 fusion.58
  150.9 1.6 fusion.58
  160.6 1.6 fusion.58
  175.2 1.6 fusion.58
  185.0 1.6 fusion.58
  189.8 1.6 fusion.58
  216.0 1.9 fusion.34
  221.6 86.1 %all-reduce.4.cloned.1.call-done = f32[128,2,8,128]{3,2,1,0:T(8,128)} async-done(((f32[128,2,8,128]{3,2,1,0:T(8,128)}), f32[128,2,8,128]{3,2,1,0:T(8,128)}) %all-reduce.4.cloned.1.call-update) | async-done | bytes 1048592 | tf_op jit(solution)/shard_map/psum | solution.py:111
  307.6 1.6 multiply_add_fusion
  309.3 106.7 %all-reduce.6.cloned.1.call-done = f32[128,128]{0,1:T(8,128)} async-done(((f32[128,128]{0,1:T(8,128)}), f32[128,128]{0,1:T(8,128)}) %all-reduce.6.cloned.1.call-update) | async-done | bytes 65552 | tf_op jit(solution)/shard_map/psum | solution.py:74
  416.0 71.8 %reduce-scatter.2.cloned.1.call-done = f32[8,8192]{1,0:T(8,128)} async-done(((f32[128,8192]{1,0:T(8,128)}), f32[8,8192]{1,0:T(8,128)}) %reduce-scatter.2.cloned.1.call-update) | async-done | bytes 262160 | tf_op jit(solution)/shard_map/reduce_scatter | solution.py:108
  487.7 2.7 fusion.8
  (215 shorter events, 145.4 us)
Async XLA Ops:
  7.2 48.0 %all-gather.2.cloned.1.call-start = ((), (), s32[]{:S(2)}) async-start(), calls=%async_computation.1 | async-start | bytes 2228224 | tf_op jit(solution)/shard_map/all_gather | solution.py:67
  7.9 299.7 %all-reduce.4.cloned.1.call-start = ((), (), s32[]{:S(2)}) async-start(), calls=%async_computation.2 | async-start | bytes 2097152 | tf_op jit(solution)/shard_map/psum | solution.py:111
  8.8 38.6 %copy-start.3 = (bf16[128,128]{1,0:T(8,128)(2,1)}, bf16[128,128]{1,0:T(8,128)(2,1)S(1)}, u32[]{:S(2)}) copy-start(bf16[128,128]{1,0:T(8,128)(2,1)S(1)} %convert_element_type.32) | copy-start | bytes 98308
  46.2 8.3 %copy-start.1 = (bf16[128,2,8,128]{3,2,1,0:T(8,128)(2,1)}, bf16[128,2,8,128]{3,2,1,0:T(8,128)(2,1)S(1)}, u32[]{:S(2)}) copy-start(bf16[128,2,8,128]{3,2,1,0:T(8,128)(2,1)S(1)} %all_gather.6) | copy-start | bytes 1572868
  46.2 8.3 %copy-start.5 = (s32[8192]{0:T(1024)S(1)}, s32[8192]{0:T(1024)}, u32[]{:S(2)}) copy-start(s32[8192]{0:T(1024)} %param.11) | copy-start | bytes 98308
  49.4 165.4 %collective-permute-start.1 = (bf16[128,1,8,128]{3,2,1,0:T(8,128)(2,1)}, bf16[128,1,8,128]{3,2,1,0:T(8,128)(2,1)S(1)}, u32[]{:S(2)}, u32[]{:S(2)}) collective-permute-start(bf16[128,1,8,128]{3,2,1,0:T(8,128)(2,1)} %get-tuple-element.170), channel_id=1, source_target_pairs={{8,0},{16,8},{24,16},{32,24},{40,32},{48,40},{56,48},{64,56},{72,6... | collective-permute-start | bytes 786440 | tf_op jit(solution)/shard_map/ppermute | solution.py:19
  50.6 164.1 %collective-permute-start = (bf16[128,1,8,128]{3,2,1,0:T(8,128)(2,1)}, bf16[128,1,8,128]{3,2,1,0:T(8,128)(2,1)}, u32[]{:S(2)}, u32[]{:S(2)}) collective-permute-start(bf16[128,1,8,128]{3,2,1,0:T(8,128)(2,1)} %get-tuple-element.169), channel_id=1, source_target_pairs={{0,8},{8,16},{16,24},{24,32},{32,40},{40,48},{48,56},{56,64},{64,7... | collective-permute-start | bytes 786440 | tf_op jit(solution)/shard_map/ppermute | solution.py:17
  213.5 1.3 copy-start.4
  214.7 201.3 %all-reduce.6.cloned.1.call-start = ((), (), s32[]{:S(2)}) async-start(), calls=%async_computation.3 | async-start | bytes 131072 | tf_op jit(solution)/shard_map/psum | solution.py:74
  216.0 1.9 copy-start.2
  218.9 268.8 %reduce-scatter.2.cloned.1.call-start = ((), (), s32[]{:S(2)}) async-start(), calls=%async_computation.4 | async-start | bytes 4456448 | tf_op jit(solution)/shard_map/reduce_scatter | solution.py:108
  218.9 1.6 copy-start
Sparse Core Ops, SparseCore 0:
  9.7 37.1 all-gather.1
  214.8 92.7 all-reduce.3
  310.7 105.2 all-reduce.5
  418.2 69.4 reduce-scatter.1
where the time goes:
time: 501 us; the launch traced here: 497 us
  waiting for transfers between devices  266 us (53%)
  matrix products  111 us (22%)
  local copies, waits for them, and re-layouts  56 us (11%)
  blocking collectives  37.5 us (7%)
  between operations  13.9 us (3%)
  other arithmetic  6.25 us (1%)
  starting transfers between devices  5.2 us (1%)
    psum x1, waiting for transfers between devices, per_device(): moment = lax.psum(moment_part, 'space')  107 us
    psum x1, waiting for transfers between devices, per_device(): k_summed = lax.psum(k_term, 'samp')  86.1 us
    reduce_scatter x1, waiting for transfers between devices, per_device(): l_proj = lax.psum_scatter(l_terms, 'space', scatter_dimension=0, tiled=True)  71.8 us
    dot_general x32, matrix products, tile_terms(): lax.dot_general(k_flat, v_block, (((0,), (0,)), ((), ())), preferred_elem...  50.6 us
    dot_general x32, matrix products, tile_terms(): lax.dot_general(v_block, reaction, (((1,), (1,)), ((), ())), preferred_el...  40.9 us
    all_gather x1, blocking collectives, per_device(): full_u = lax.all_gather(basis_u, 'samp', axis=0, tiled=True)  37.5 us
    dynamic_update_slice x64, local copies, waits for them, and re-layouts, turn_after(): l_terms = lax.dynamic_update_slice_in_dim(l_terms, l_term, offset, 1)  24.9 us
    dynamic_slice x32, local copies, waits for them, and re-layouts, tile_terms(): g_block = lax.dynamic_slice_in_dim(growth, offset, block_rows, 0)  24.3 us
  transfers between devices with their start and end apart: 6, of which 3 were waited for; matrix products, arithmetic and copies ran while one was open for 34% of the time, Pallas kernels for 0%

commit v1 on v0

v1 whole, which is shorter than its diff:
```python
import functools

import jax
import jax.numpy as jnp
from jax import lax
from jax.experimental import pallas as pl
from jax.experimental.pallas import tpu as pltpu
from jax.sharding import Mesh, PartitionSpec as P

step_size = 0.1
SPACE = ("z", "xl", "c")
SAMP = ("y", "xh")
CHUNKS = 2
bf16, f32 = jnp.bfloat16, jnp.float32


def dot(a, b, ca, cb):
    return lax.dot_general(a, b, (((ca,), (cb,)), ((), ())), preferred_element_type=f32)


def whole(shape):
    return pl.BlockSpec(shape, lambda *_: (0,) * len(shape))


def call(body, outs, grid=None, in_specs=None, out_specs=None, **kw):
    extra = {}
    if grid is not None:
        extra = dict(grid=grid, in_specs=in_specs, out_specs=out_specs)
    return pl.pallas_call(
        body,
        out_shape=[jax.ShapeDtypeStruct(s, d) for s, d in outs],
        compiler_params=pltpu.CompilerParams(vmem_limit_bytes=56 << 20),
        **extra,
        **kw,
    )


def prep_body(c_ref, own_ref, oth_ref, core_ref, k_ref, ko_ref, kt_ref, halo_ref):
    core_b = core_ref[...].astype(bf16)
    cells = own_ref.shape[1]
    half = cells // 2
    k_own = dot(core_b, own_ref[...], 0, 0).astype(bf16)
    k_oth = dot(core_b, oth_ref[...], 0, 0).astype(bf16)
    k_ref[...] = k_own
    kt_ref[:cells, :] = k_own.T
    kt_ref[cells:, :] = k_oth.T
    first = c_ref[0] == 0

    @pl.when(first)
    def _():
        halo_ref[...] = k_own[:, :half]
        ko_ref[...] = k_oth[:, :half]

    @pl.when(jnp.logical_not(first))
    def _():
        halo_ref[...] = k_own[:, half:]
        ko_ref[...] = k_oth[:, half:]


def lap_body(rows, cols, c_ref, k_ref, near_ref, halo_ref, face_ref, u_ref, base_ref, m_ref, base_s, lap_s):
    first = c_ref[0] == 0
    near = near_ref[...].astype(f32)
    halo = halo_ref[...].astype(f32)
    before = jnp.where(first, halo, near)
    after = jnp.where(first, near, halo)
    plane = rows * cols
    lane = lax.broadcasted_iota(jnp.int32, (1, cols), 1)
    for x in range(2):
        for y in range(rows):
            at = (x * rows + y) * cols
            mid = k_ref[:, at : at + cols].astype(f32)
            w = [0.25 * lax.shift_left(1, face_ref[f, x, y : y + 1, :]).astype(f32) for f in range(6)]
            total = ((w[0] + w[1]) + (w[2] + w[3])) + (w[4] + w[5])
            down = before[:, y * cols : (y + 1) * cols] if x == 0 else k_ref[:, at - plane : at - plane + cols].astype(f32)
            up = after[:, y * cols : (y + 1) * cols] if x == 1 else k_ref[:, at + plane : at + plane + cols].astype(f32)
            out = w[0] * down + w[1] * up - total * mid
            if y > 0:
                out += w[2] * k_ref[:, at - cols : at].astype(f32)
            if y < rows - 1:
                out += w[3] * k_ref[:, at + cols : at + 2 * cols].astype(f32)
            out += jnp.where(lane == 0, 0.0, w[4]) * pltpu.roll(mid, 1, 1)
            out += jnp.where(lane == cols - 1, 0.0, w[5]) * pltpu.roll(mid, cols - 1, 1)
            base_s[:, at : at + cols] = mid + step_size * out
            lap_s[:, at : at + cols] = out.astype(bf16)
    base_ref[...] = base_s[pl.ds(pl.multiple_of(c_ref[1] * base_ref.shape[0], 8), base_ref.shape[0]), :]
    m_ref[...] = dot(u_ref[...], lap_s[...], 1, 1)


def main_body(tile, scale, first, *refs):
    if first:
        kt_ref, own_ref, oth_ref, v_ref, g_ref, ma_ref, mb_ref, core_ref, l_ref, ov_ref, w_s = refs
    else:
        kt_ref, own_ref, oth_ref, v_ref, g_ref, ma_ref, mb_ref, core_ref, old_ref, l_ref, ov_ref, w_s = refs
    step = pl.program_id(0)
    rank = v_ref.shape[0]

    @pl.when(step == 0)
    def _():
        ov_ref[...] = jnp.zeros_like(ov_ref) if first else old_ref[...]
        w = core_ref[...].astype(bf16).astype(f32) * 0.125 + scale * (ma_ref[...] + mb_ref[...])
        high = w.astype(bf16)
        w_s[:rank, :] = high
        w_s[rank:, :] = (w - high.astype(f32)).astype(bf16)

    v = v_ref[...]
    g = g_ref[...]
    acc = None
    cells = own_ref.shape[1]
    for u_ref, base in ((own_ref, 0), (oth_ref, cells)):
        for at in range(0, cells, tile):
            field = dot(kt_ref[base + at : base + at + tile, :], v, 1, 0)
            react = (field * (g - field * field)).astype(bf16)
            ov_ref[base + at : base + at + tile, :] += dot(react, v, 1, 1)
            part = dot(u_ref[:, at : at + tile], react, 1, 0)
            acc = part if acc is None else acc + part
    side = dot(w_s[...], v, 1, 0)
    l_ref[...] = (scale * acc + (side[:rank] + side[rank:])).astype(bf16)


def turn_body(ov_ref, own_ref, oth_ref):
    cells = own_ref.shape[1]
    own_ref[...] = ov_ref[:cells, :].T
    oth_ref[...] = ov_ref[cells:, :].T.astype(bf16)


def spread(x, axes, parts):
    wide = jnp.broadcast_to(x[None], (parts,) + x.shape)
    wide = wide.reshape((parts * x.shape[0],) + x.shape[1:])
    return lax.all_to_all(wide, axes, 0, 0, tiled=True)


def per_device(basis_u, basis_v, core_s, face_class, sample_class):
    narrow, depth_x, rows_y, cols_z = basis_u.shape
    rank = core_s.shape[0]
    n_samp, n_space = 8, 16
    cells = depth_x * rows_y * cols_z
    lanes, samp_rows = basis_v.shape
    half = samp_rows // 2
    width = half // CHUNKS
    cell_weight = rank / (cells * n_space)
    samp_weight = rank / (samp_rows * n_samp)
    core_at = lax.axis_index("c")
    samp_at = lax.axis_index(SAMP)
    where_at = jnp.stack([core_at, samp_at]).astype(jnp.int32)
    swap = [(0, 1), (1, 0)]

    u_own = spread(basis_u.reshape(narrow, cells), SAMP, n_samp)
    v_parts = []
    v_half = basis_v.reshape(lanes, 2, CHUNKS, width)
    for j in range(CHUNKS):
        pair = jnp.transpose(v_half[:, :, j], (1, 0, 2))
        v_parts.append(spread(pair.reshape(2 * lanes, width), SPACE, n_space // 2))
    u_oth = lax.ppermute(u_own, "c", swap)

    smem = pl.BlockSpec(memory_space=pltpu.SMEM)
    vm = pl.BlockSpec(memory_space=pltpu.VMEM)
    k_own, near, kt, send = pl.pallas_call(
        prep_body,
        in_specs=[smem, vm, vm, vm],
        out_shape=[
            jax.ShapeDtypeStruct((rank, cells), bf16),
            jax.ShapeDtypeStruct((rank, cells // 2), bf16),
            jax.ShapeDtypeStruct((2 * cells, rank), bf16),
            jax.ShapeDtypeStruct((rank, cells // 2), bf16),
        ],
    )(where_at, u_own, u_oth, core_s)
    chips = n_space // 2
    hops = [(2 * i + 1, 2 * i + 2) for i in range(chips - 1)] + [(2 * i + 2, 2 * i + 1) for i in range(chips - 1)]
    halo = lax.ppermute(send, SPACE, hops)
    base, m_own = pl.pallas_call(
        functools.partial(lap_body, rows_y, cols_z),
        in_specs=[smem] + [vm] * 5,
        out_shape=[jax.ShapeDtypeStruct((narrow, cells), f32), jax.ShapeDtypeStruct((rank, rank), f32)],
        scratch_shapes=[pltpu.VMEM((rank, cells), f32), pltpu.VMEM((rank, cells), bf16)],
    )(where_at, k_own, near, halo, face_class, u_own)
    m_oth = lax.ppermute(m_own, "c", swap)

    growth = 0.5 + 0.5 * lax.dynamic_slice_in_dim(sample_class, core_at * half, half, 0).astype(f32)
    growth = growth.reshape(CHUNKS, 1, width)
    block = min(1024, width)
    ov = None
    l_parts = []
    for j in range(CHUNKS):
        first = j == 0
        ins = [kt, u_own, u_oth, v_parts[j], growth[j], m_own, m_oth, core_s] + ([] if first else [ov])
        specs = [
            whole(kt.shape),
            whole(u_own.shape),
            whole(u_oth.shape),
            pl.BlockSpec((rank, block), lambda i: (0, i)),
            pl.BlockSpec((1, block), lambda i: (0, i)),
            whole((rank, rank)),
            whole((rank, rank)),
            whole((rank, rank)),
        ] + ([] if first else [whole((2 * cells, rank))])
        l_part, ov = call(
            functools.partial(main_body, 512, step_size * cell_weight, first),
            [((rank, width), bf16), ((2 * cells, rank), f32)],
            grid=(width // block,),
            in_specs=specs,
            out_specs=[pl.BlockSpec((rank, block), lambda i: (0, i)), whole((2 * cells, rank))],
            scratch_shapes=[pltpu.VMEM((2 * rank, rank), bf16)],
        )(*ins)
        got = lax.all_to_all(l_part, SPACE, 0, 0, tiled=True)
        l_parts.append(got.reshape(n_space // 2, 2, lanes, width).astype(f32).sum(0))
    l_new = jnp.stack(l_parts, 2)
    l_new = jnp.transpose(l_new, (1, 0, 2, 3)).reshape(lanes, samp_rows)

    ov_own, ov_send = call(turn_body, [((rank, cells), f32), ((rank, cells), bf16)])(ov)
    ov_sum = (ov_own + lax.ppermute(ov_send, "c", swap).astype(f32)).astype(bf16)
    k_got = lax.all_to_all(ov_sum, SAMP, 0, 0, tiled=True)
    k_sum = k_got.reshape(n_samp, narrow, cells).astype(f32).sum(0)
    k_new = base + (step_size * samp_weight) * k_sum
    return (k_new.reshape(basis_u.shape), l_new)


def solution(mesh):
    fine = Mesh(mesh.devices.reshape(4, 2, 2, 4, 2), SPACE + SAMP)
    return jax.shard_map(
        per_device,
        mesh=fine,
        in_specs=(P(SAMP, SPACE, None, None), P(SPACE, SAMP), P(), P(None, SPACE, None, None), P(SAMP)),
        out_specs=(P(SAMP, SPACE, None, None), P(SPACE, SAMP)),
        check_vma=False,
    )
```

time: 501 us -> 145 us (0.29)
  waiting for transfers between devices: 266 us -> 41.8 us
  matrix products: 111 us -> 0 us
  local copies, waits for them, and re-layouts: 56 us -> 8.66 us
  Pallas kernels: 0 us -> 39.1 us
  starting transfers between devices: 5.2 us -> 34 us
  blocking collectives: 37.5 us -> 17.2 us
  between operations: 13.9 us -> 0.78 us
    psum x2 -> x0, waiting for transfers between devices: 193 us -> none  [the longest x1 107 us: per_device(): moment = lax.psum(moment_part, 'space')]
    dot_general x100 -> x0, matrix products: 111 us -> none  [the longest x32 50.6 us: tile_terms(): lax.dot_general(k_flat, v_block, (((0,), (0,)), ((), ())), preferred_elem...]
    reduce_scatter x1 -> x0, waiting for transfers between devices: 71.8 us -> none  [per_device(): l_proj = lax.psum_scatter(l_terms, 'space', scatter_dimension=0, tiled=True)]
    all_to_all x0 -> x5, waiting for transfers between devices: none -> 41.3 us  [the longest x3 21.1 us: spread(): return lax.all_to_all(wide, axes, 0, 0, tiled=True)]
    pallas_call x0 -> x5, Pallas kernels: none -> 39.1 us  [the longest x2 29.7 us: per_device(): call(functools.partial(main_body, 512, step_size * cell_weight, first), [...]
    all_gather x1 -> x0, blocking collectives: 37.5 us -> none  [per_device(): full_u = lax.all_gather(basis_u, 'samp', axis=0, tiled=True)]
    dynamic_update_slice x64 -> x0, local copies, waits for them, and re-layouts: 24.9 us -> none  [turn_after(): l_terms = lax.dynamic_update_slice_in_dim(l_terms, l_term, offset, 1)]
    dynamic_slice x32 -> x0, local copies, waits for them, and re-layouts: 24.3 us -> none  [tile_terms(): g_block = lax.dynamic_slice_in_dim(growth, offset, block_rows, 0)]
  transfers between devices with their start and end apart: 6 -> 9, of which waited for: 3 -> 5; matrix products, arithmetic and copies ran while one was open for 34% -> 3% of each run, Pallas kernels for 0% -> 14%
where the time goes in v1:
time: 145 us; the launch traced here: 144 us
  waiting for transfers between devices  41.8 us (29%)
  Pallas kernels  39.1 us (27%)
  starting transfers between devices  34 us (23%)
  blocking collectives  17.2 us (12%)
  local copies, waits for them, and re-layouts  8.66 us (6%)
  other arithmetic  2.5 us (2%)
    pallas_call x2, Pallas kernels, per_device(): call(functools.partial(main_body, 512, step_size * cell_weight, first), [...  29.7 us
    all_to_all x3, waiting for transfers between devices, spread(): return lax.all_to_all(wide, axes, 0, 0, tiled=True)  21.1 us
    all_to_all x1, blocking collectives, per_device(): got = lax.all_to_all(l_part, SPACE, 0, 0, tiled=True)  17.2 us
    all_to_all x3, starting transfers between devices, spread(): return lax.all_to_all(wide, axes, 0, 0, tiled=True)  16.1 us
    all_to_all x1, waiting for transfers between devices, per_device(): k_got = lax.all_to_all(ov_sum, SAMP, 0, 0, tiled=True)  10.3 us
    all_to_all x1, waiting for transfers between devices, per_device(): got = lax.all_to_all(l_part, SPACE, 0, 0, tiled=True)  9.86 us
    ppermute x1, starting transfers between devices, per_device(): m_oth = lax.ppermute(m_own, 'c', swap)  9.49 us
    unnamed x22, local copies, waits for them, and re-layouts  4.46 us
  transfers between devices with their start and end apart: 9, of which 5 were waited for; matrix products, arithmetic and copies ran while one was open for 3% of the time, Pallas kernels for 14%

profile of v1, /device:TPU:0, one launch (start us, length us, event | category | flops | bytes accessed | tf_op | source)
XLA Modules:
  0.0 144.1 jit_solution(1372335921449314942)
XLA Ops:
  0.6 0.9 copy.10
  1.5 0.9 broadcast_in_dim.22
  2.3 7.0 %all-to-all-start = ((bf16[8,16,2048]{2,1,0:T(8,128)(2,1)}), bf16[8,16,2048]{2,1,0:T(8,128)(2,1)S(1)}, u32[]{:S(2)}, u32[]{:S(2)}) async-start(bf16[8,16,2048]{2,1,0:T(8,128)(2,1)} %broadcast_in_dim.22), calls=%async_computation | async-start | bytes 1048576 | tf_op jit(solution)/shard_map/all_to_all | solution.py:129
  9.4 0.9 slice_bitcast_fusion
  10.3 10.7 %all-to-all-done = bf16[8,16,2048]{2,1,0:T(8,128)(2,1)S(1)} async-done(((bf16[8,16,2048]{2,1,0:T(8,128)(2,1)}), bf16[8,16,2048]{2,1,0:T(8,128)(2,1)S(1)}, u32[]{:S(2)}, u32[]{:S(2)}) %all-to-all-start) | async-done | bytes 524320 | tf_op jit(solution)/shard_map/all_to_all | solution.py:129
  21.0 1.0 broadcast_in_dim.26
  21.9 5.4 %all-to-all-start.2 = ((bf16[16,8,2048]{2,1,0:T(8,128)(2,1)}), bf16[16,8,2048]{2,1,0:T(8,128)(2,1)S(1)}, u32[]{:S(2)}, u32[]{:S(2)}) async-start(bf16[16,8,2048]{2,1,0:T(8,128)(2,1)} %bitcast.13), calls=%async_computation.2 | async-start | bytes 1048576 | tf_op jit(solution)/shard_map/all_to_all | solution.py:129
  27.8 10.4 %all-to-all-done.2 = bf16[16,8,2048]{2,1,0:T(8,128)(2,1)S(1)} async-done(((bf16[16,8,2048]{2,1,0:T(8,128)(2,1)}), bf16[16,8,2048]{2,1,0:T(8,128)(2,1)S(1)}, u32[]{:S(2)}, u32[]{:S(2)}) %all-to-all-start.2) | async-done | bytes 524320 | tf_op jit(solution)/shard_map/all_to_all | solution.py:129
  38.2 0.9 broadcast_in_dim.24
  39.1 3.6 %all-to-all-start.1 = ((bf16[16,8,2048]{2,1,0:T(8,128)(2,1)}), bf16[16,8,2048]{2,1,0:T(8,128)(2,1)S(1)}, u32[]{:S(2)}, u32[]{:S(2)}) async-start(bf16[16,8,2048]{2,1,0:T(8,128)(2,1)} %bitcast.7), calls=%async_computation.1 | async-start | bytes 1048576 | tf_op jit(solution)/shard_map/all_to_all | solution.py:129
  43.3 0.8 copy-done.1
  44.1 3.1 %shard_map.68 = (bf16[128,2048]{1,0:T(8,128)(2,1)}, bf16[128,1024]{1,0:T(8,128)(2,1)}, bf16[4096,128]{1,0:T(8,128)(2,1)}, bf16[128,1024]{1,0:T(8,128)(2,1)}) custom-call(s32[2]{0:T(128)} %pad_add_fusion.c_ref, bf16[128,2048]{1,0:T(8,128)(2,1)} %bitcast.44, bf16[128,2048]{1,0:T(8,128)(2,1)} %copy-done.1, f32[128,128]{1,0:T(8,128)} %refs_7_.3), custom_call_target="tpu_custom_call" | custom-call | tf_op jit(solution)/shard_map/pallas_call | solution.py:157
  48.6 3.1 %shard_map.69 = (f32[16,2048]{1,0:T(8,128)}, f32[128,128]{1,0:T(8,128)}) custom-call(s32[2]{0:T(128)} %pad_add_fusion.c_ref, bf16[128,2048]{1,0:T(8,128)(2,1)} %get-tuple-element.14.k_ref, bf16[128,1024]{1,0:T(8,128)(2,1)} %get-tuple-element.15.near_ref, bf16[128,1024]{1,0:T(8,128)(2,1)} %copy-done.7, s32[6,2,8,128]{3,2,1,0:T(8,128)} %face_ref.1, ...), custom_call_target="tpu_custom_call" | custom-call | tf_op jit(solution)/shard_map/pallas_call | solution.py:170
  51.8 9.5 %collective-permute-start.2 = (f32[128,128]{1,0:T(8,128)}, f32[128,128]{1,0:T(8,128)S(1)}, u32[]{:S(2)}, u32[]{:S(2)}) collective-permute-start(f32[128,128]{1,0:T(8,128)} %get-tuple-element.19.refs_5_), channel_id=1, source_target_pairs={{0,8},{8,0},{1,9},{9,1},{2,10},{10,2},{3,11},{11,3},{4,12},{12,4},... | collective-permute-start | bytes 196616 | tf_op jit(solution)/shard_map/ppermute | solution.py:176
  63.0 14.5 %shard_map.70 = (bf16[128,2048]{1,0:T(8,128)(2,1)}, f32[4096,128]{1,0:T(8,128)}) custom-call(bf16[4096,128]{1,0:T(8,128)(2,1)} %get-tuple-element.18.refs_0_, bf16[128,2048]{1,0:T(8,128)(2,1)} %bitcast.46, bf16[128,2048]{1,0:T(8,128)(2,1)} %copy-done.1, bf16[128,2048]{1,0:T(8,128)(2,1)} %bitcast.51, f32[1,2048]{1,0:T(1,128)} %bitcast.61, ...), custom_call_target="tpu_custom_call" | custom-call | tf_op jit(solution)/shard_map/pallas_call | solution.py:196
  77.5 0.8 copy-done.2
  78.3 15.2 %shard_map.71 = (bf16[128,2048]{1,0:T(8,128)(2,1)}, f32[4096,128]{1,0:T(8,128)}) custom-call(bf16[4096,128]{1,0:T(8,128)(2,1)} %get-tuple-element.18.refs_0_, bf16[128,2048]{1,0:T(8,128)(2,1)} %bitcast.47, bf16[128,2048]{1,0:T(8,128)(2,1)} %copy-done.1, bf16[128,2048]{1,0:T(8,128)(2,1)} %bitcast.48, f32[1,2048]{1,0:T(1,128)} %bitcast.60, ...), custom_call_target="tpu_custom_call" | custom-call | tf_op jit(solution)/shard_map/pallas_call | solution.py:196
  93.5 3.1 %shard_map.72 = (f32[128,2048]{1,0:T(8,128)}, bf16[128,2048]{1,0:T(8,128)(2,1)}) custom-call(f32[4096,128]{1,0:T(8,128)} %get-tuple-element.21.ov_ref), custom_call_target="tpu_custom_call" | custom-call | tf_op jit(solution)/shard_map/pallas_call | solution.py:209
  97.0 17.2 %all_to_all.57 = bf16[16,8,2048]{2,1,0:T(8,128)(2,1)S(1)} all-to-all(bf16[16,8,2048]{2,1,0:T(8,128)(2,1)S(1)} %bitcast.52), channel_id=1, replica_groups=mesh['z'=4,'xl'=2,'c'=2,'y'=4,'xh'=2] {'z','xl','c'}, dimensions={0} | all-to-all | bytes 1048576 | tf_op jit(solution)/shard_map/all_to_all | solution.py:204
  114.2 3.6 %all-to-all-start.5 = ((bf16[16,8,2048]{2,1,0:T(8,128)(2,1)}), bf16[16,8,2048]{2,1,0:T(8,128)(2,1)S(1)}, u32[]{:S(2)}, u32[]{:S(2)}) async-start(bf16[16,8,2048]{2,1,0:T(8,128)(2,1)} %bitcast.20), calls=%async_computation.5 | async-start | bytes 1048576 | tf_op jit(solution)/shard_map/all_to_all | solution.py:204
  117.8 0.9 add_convert_fusion
  118.7 9.9 %all-to-all-done.5 = bf16[16,8,2048]{2,1,0:T(8,128)(2,1)S(1)} async-done(((bf16[16,8,2048]{2,1,0:T(8,128)(2,1)}), bf16[16,8,2048]{2,1,0:T(8,128)(2,1)S(1)}, u32[]{:S(2)}, u32[]{:S(2)}) %all-to-all-start.5) | async-done | bytes 524320 | tf_op jit(solution)/shard_map/all_to_all | solution.py:204
  128.6 3.5 %all-to-all-start.3 = ((bf16[8,16,2048]{2,1,0:T(8,128)(2,1)}), bf16[8,16,2048]{2,1,0:T(8,128)(2,1)S(1)}, u32[]{:S(2)}, u32[]{:S(2)}) async-start(bf16[8,16,2048]{2,1,0:T(8,128)(2,1)} %bitcast.16), calls=%async_computation.3 | async-start | bytes 1048576 | tf_op jit(solution)/shard_map/all_to_all | solution.py:211
  133.0 10.3 %all-to-all-done.3 = bf16[8,16,2048]{2,1,0:T(8,128)(2,1)S(1)} async-done(((bf16[8,16,2048]{2,1,0:T(8,128)(2,1)}), bf16[8,16,2048]{2,1,0:T(8,128)(2,1)S(1)}, u32[]{:S(2)}, u32[]{:S(2)}) %all-to-all-start.3) | async-done | bytes 524320 | tf_op jit(solution)/shard_map/all_to_all | solution.py:211
  (35 shorter events, 6.2 us)
Async XLA Ops:
  2.3 18.6 %all-to-all-start = ((bf16[8,16,2048]{2,1,0:T(8,128)(2,1)}), bf16[8,16,2048]{2,1,0:T(8,128)(2,1)S(1)}, u32[]{:S(2)}, u32[]{:S(2)}) async-start(bf16[8,16,2048]{2,1,0:T(8,128)(2,1)} %broadcast_in_dim.22), calls=%async_computation | async-start | bytes 1048576 | tf_op jit(solution)/shard_map/all_to_all | solution.py:129
  21.0 22.4 %copy-start = (bf16[8,16,2048]{2,1,0:T(8,128)(2,1)}, bf16[8,16,2048]{2,1,0:T(8,128)(2,1)S(1)}, u32[]{:S(2)}) copy-start(bf16[8,16,2048]{2,1,0:T(8,128)(2,1)S(1)} %all-to-all-done) | copy-start | bytes 1572868
  21.0 26.9 %copy-start.9 = (s32[8192]{0:T(1024)S(1)}, s32[8192]{0:T(1024)}, u32[]{:S(2)}) copy-start(s32[8192]{0:T(1024)} %param.9) | copy-start | bytes 98308
  21.9 16.3 %all-to-all-start.2 = ((bf16[16,8,2048]{2,1,0:T(8,128)(2,1)}), bf16[16,8,2048]{2,1,0:T(8,128)(2,1)S(1)}, u32[]{:S(2)}, u32[]{:S(2)}) async-start(bf16[16,8,2048]{2,1,0:T(8,128)(2,1)} %bitcast.13), calls=%async_computation.2 | async-start | bytes 1048576 | tf_op jit(solution)/shard_map/all_to_all | solution.py:129
  27.4 15.9 %collective-permute-start = (bf16[128,2048]{1,0:T(8,128)(2,1)S(1)}, bf16[128,2048]{1,0:T(8,128)(2,1)S(1)}, u32[]{:S(2)}, u32[]{:S(2)}) collective-permute-start(bf16[128,2048]{1,0:T(8,128)(2,1)S(1)} %bitcast.43), channel_id=1, source_target_pairs={{0,8},{8,0},{1,9},{9,1},{2,10},{10,2},{3,11},{11,3},{4,12},{12,4},... | collective-permute-start | bytes 1572872 | tf_op jit(solution)/shard_map/ppermute | solution.py:153
  38.2 13.5 %copy-start.3 = (bf16[16,8,2048]{2,1,0:T(8,128)(2,1)}, bf16[16,8,2048]{2,1,0:T(8,128)(2,1)S(1)}, u32[]{:S(2)}) copy-start(bf16[16,8,2048]{2,1,0:T(8,128)(2,1)S(1)} %all-to-all-done.2) | copy-start | bytes 1572868
  39.1 38.4 %all-to-all-start.1 = ((bf16[16,8,2048]{2,1,0:T(8,128)(2,1)}), bf16[16,8,2048]{2,1,0:T(8,128)(2,1)S(1)}, u32[]{:S(2)}, u32[]{:S(2)}) async-start(bf16[16,8,2048]{2,1,0:T(8,128)(2,1)} %bitcast.7), calls=%async_computation.1 | async-start | bytes 1048576 | tf_op jit(solution)/shard_map/all_to_all | solution.py:129
  43.3 0.8 copy-start.1
  47.2 0.7 collective-permute-start.1
  47.9 0.7 copy-start.7
  51.8 10.6 %collective-permute-start.2 = (f32[128,128]{1,0:T(8,128)}, f32[128,128]{1,0:T(8,128)S(1)}, u32[]{:S(2)}, u32[]{:S(2)}) collective-permute-start(f32[128,128]{1,0:T(8,128)} %get-tuple-element.19.refs_5_), channel_id=1, source_target_pairs={{0,8},{8,0},{1,9},{9,1},{2,10},{10,2},{3,11},{11,3},{4,12},{12,4},... | collective-permute-start | bytes 196616 | tf_op jit(solution)/shard_map/ppermute | solution.py:176
  62.4 0.6 copy-start.6
  77.5 0.8 copy-start.2
  93.5 3.5 %copy-start.5 = (bf16[128,2048]{1,0:T(8,128)(2,1)S(1)}, bf16[128,2048]{1,0:T(8,128)(2,1)}, u32[]{:S(2)}) copy-start(bf16[128,2048]{1,0:T(8,128)(2,1)} %get-tuple-element.24) | copy-start | bytes 1572868
  96.6 21.2 %copy-start.4 = (f32[128,2048]{1,0:T(8,128)S(1)}, f32[128,2048]{1,0:T(8,128)}, u32[]{:S(2)}) copy-start(f32[128,2048]{1,0:T(8,128)} %get-tuple-element.22) | copy-start | bytes 3145732
  96.6 21.1 %collective-permute-start.3 = (bf16[128,2048]{1,0:T(8,128)(2,1)}, bf16[128,2048]{1,0:T(8,128)(2,1)S(1)}, u32[]{:S(2)}, u32[]{:S(2)}) collective-permute-start(bf16[128,2048]{1,0:T(8,128)(2,1)} %get-tuple-element.23), channel_id=1, source_target_pairs={{0,8},{8,0},{1,9},{9,1},{2,10},{10,2},{3,11},{11,3},{4,12},{12,4},... | collective-permute-start | bytes 1572872 | tf_op jit(solution)/shard_map/ppermute | solution.py:210
  114.2 14.4 %all-to-all-start.5 = ((bf16[16,8,2048]{2,1,0:T(8,128)(2,1)}), bf16[16,8,2048]{2,1,0:T(8,128)(2,1)S(1)}, u32[]{:S(2)}, u32[]{:S(2)}) async-start(bf16[16,8,2048]{2,1,0:T(8,128)(2,1)} %bitcast.20), calls=%async_computation.5 | async-start | bytes 1048576 | tf_op jit(solution)/shard_map/all_to_all | solution.py:204
  118.7 24.7 %copy-start.8 = (f32[16,2048]{1,0:T(8,128)S(1)}, f32[16,2048]{1,0:T(8,128)}, u32[]{:S(2)}) copy-start(f32[16,2048]{1,0:T(8,128)} %get-tuple-element.17) | copy-start | bytes 393220
  128.6 14.7 %all-to-all-start.3 = ((bf16[8,16,2048]{2,1,0:T(8,128)(2,1)}), bf16[8,16,2048]{2,1,0:T(8,128)(2,1)S(1)}, u32[]{:S(2)}, u32[]{:S(2)}) async-start(bf16[8,16,2048]{2,1,0:T(8,128)(2,1)} %bitcast.16), calls=%async_computation.3 | async-start | bytes 1048576 | tf_op jit(solution)/shard_map/all_to_all | solution.py:211
